TPU v7x, 128 devices: a whole 4x4x4 slice. The times are simulated.
128 devices in a mesh: ctx: 8 (over y_hi, z), exp: 16 (over y_lo, x, core).
Axes of the slice: x: 4, y: 4 (y_hi: 2, y_lo: 2; y = y_hi * 2 + y_lo), z: 4, core: 2. Of those that a mesh axis runs over, the one named last changes fastest.
Arguments:
- moe_input: bfloat16 [16384, 4096], P(('ctx', 'exp')), may hold values from -6 to 6
- out_grad: bfloat16 [16384, 4096], P(('ctx', 'exp')), may hold values from -6 to 6
- w_gate: bfloat16 [32, 4096, 1408], P('exp', None, 'ctx'), may hold values from -0.09375 to 0.09375
- w_up: bfloat16 [32, 4096, 1408], P('exp', None, 'ctx'), may hold values from -0.09375 to 0.09375
- w_down: bfloat16 [32, 1408, 4096], P('exp', 'ctx'), may hold values from -0.15625 to 0.15625
- expert_picks: int32 [32, 128], replicated, may hold values from 0 to 16383, as said below
- gate_probs: float32 [32, 128], replicated, may hold values from 0.2 to 1
- queries: bfloat16 [16384, 2048], P('ctx', 'exp'), may hold values from -6 to 6
- attn_keys: bfloat16 [16384, 2048], P('ctx', 'exp'), may hold values from -6 to 6
- values: bfloat16 [16384, 2048], P('ctx', 'exp'), may hold values from -6 to 6
- attn_out: bfloat16 [16384, 2048], P('ctx', 'exp'), may hold values from -1.5 to 1.5
- log_norm: float32 [16, 16384], P('exp'), may hold values from -1 to 12
- w_out: bfloat16 [2048, 4096], P('exp'), may hold values from -0.09375 to 0.09375
Outputs:
- d_resid: bfloat16 [16384, 4096], P(('ctx', 'exp'))
- dw_gate: bfloat16 [32, 4096, 1408], P('exp', None, 'ctx')
- dw_up: bfloat16 [32, 4096, 1408], P('exp', None, 'ctx')
- dw_down: bfloat16 [32, 1408, 4096], P('exp', 'ctx')
- d_gates: float32 [32, 128], P('exp', 'ctx')
- dw_out: bfloat16 [2048, 4096], P('exp', 'ctx')
- grad_q: bfloat16 [16384, 2048], P('ctx', 'exp')
- grad_k: bfloat16 [16384, 2048], P('ctx', 'exp')
- grad_v: bfloat16 [16384, 2048], P('ctx', 'exp')
Inputs may be any that keep to these rules, and one draw needn't show every extreme that they name: expert_picks[e] lists distinct tokens in ascending order: exactly 16 from each context group of 2048 consecutive tokens and at most 2 from each aligned block of 128 tokens; in every group some block gives exactly 2.
All inputs are finite; a program needn't handle non-finite values.
Results may differ from a plain program's by a relative error of at most 0.023.
Values may be sent and summed in bfloat16 or wider, within the bound.
A program may use at most 256 MiB of HBM per device.

v0:
```python
import math
import jax
import jax.numpy as jnp
from jax import lax
from jax.sharding import PartitionSpec as P

MOST = 2


def activation(pre_act):
    sigmoid_val = jax.nn.sigmoid(pre_act)
    return (pre_act * sigmoid_val, sigmoid_val * (1.0 + pre_act * (1.0 - sigmoid_val)))


def settle(value):
    return lax.optimization_barrier(value.astype(jnp.bfloat16)).astype(jnp.float32)


def contract_first(left, right):
    return lax.dot_general(
        left, right, (((0,), (0,)), ((), ())), preferred_element_type=jnp.float32
    )


def contract_last(left, right):
    return lax.dot_general(
        left, right, (((1,), (1,)), ((), ())), preferred_element_type=jnp.float32
    )


def tile_grads(
    q_rows, do_rows, norm_rows, delta_rows, keys_here, values_here, key_pos, key_scale, piece_count
):
    row_count, head_dim = q_rows.shape
    block_rows = math.gcd(row_count, 2048)
    block_total = row_count // block_rows
    piece_len = keys_here.shape[0] // piece_count

    def one_block(block_idx, carried):
        grad_rows, grad_keys, grad_values = carried
        row_start = block_idx * block_rows
        q_block = lax.dynamic_slice_in_dim(q_rows, row_start, block_rows, 0)
        do_block = lax.dynamic_slice_in_dim(do_rows, row_start, block_rows, 0)
        norm_block = lax.dynamic_slice_in_dim(norm_rows, row_start, block_rows, 0)
        delta_block = lax.dynamic_slice_in_dim(delta_rows, row_start, block_rows, 0)
        q_positions = row_start + jnp.arange(block_rows, dtype=jnp.int32)
        last_query = row_start + block_rows - 1
        keys_piece = keys_here
        values_piece = values_here
        pos_piece = key_pos

        def compute_tile(
            unused, keys_piece=keys_piece, values_piece=values_piece, pos_piece=pos_piece
        ):
            scores = contract_last(q_block, keys_piece) * key_scale
            causal = pos_piece[None, :] <= q_positions[:, None]
            attn_probs = jnp.exp(jnp.where(causal, scores - norm_block[:, None], -1e30))
            d_probs = contract_last(do_block, values_piece)
            d_scores = (attn_probs * (d_probs - delta_block[:, None])).astype(jnp.bfloat16)
            probs_low = attn_probs.astype(jnp.bfloat16)
            piece_q = jnp.dot(d_scores, keys_piece, preferred_element_type=jnp.float32) * key_scale
            piece_k = contract_first(d_scores, q_block) * key_scale
            piece_v = contract_first(probs_low, do_block)
            return (piece_q, piece_k, piece_v)

        def skip_tile(unused):
            return (
                jnp.zeros((block_rows, head_dim), jnp.float32),
                jnp.zeros((piece_len, head_dim), jnp.float32),
                jnp.zeros((piece_len, head_dim), jnp.float32),
            )

        piece_q, piece_k, piece_v = lax.cond(
            last_query >= jnp.min(pos_piece), compute_tile, skip_tile, 0
        )
        key_parts = [piece_k]
        value_parts = [piece_v]
        add_k = jnp.concatenate(key_parts, axis=0)
        add_v = jnp.concatenate(value_parts, axis=0)
        grad_rows = lax.dynamic_update_slice_in_dim(grad_rows, piece_q, row_start, 0)
        return (grad_rows, grad_keys + add_k, grad_values + add_v)

    start_state = (
        jnp.zeros((row_count, head_dim), jnp.float32),
        jnp.zeros(keys_here.shape, jnp.float32),
        jnp.zeros(values_here.shape, jnp.float32),
    )
    return lax.fori_loop(0, block_total, one_block, start_state)


def body(
    moe_input,
    out_grad,
    w_gate,
    w_up,
    w_down,
    expert_picks,
    gate_probs,
    queries,
    attn_keys,
    values,
    attn_out,
    log_norm,
    w_out,
):
    n_ctx = lax.axis_size("ctx")
    n_exp = lax.axis_size("exp")
    ctx_id = lax.axis_index("ctx")
    exp_id = lax.axis_index("exp")
    tok_dev, feat_width = moe_input.shape
    n_local = w_gate.shape[0]
    slot_count = MOST
    group_picks = expert_picks.shape[1] // n_ctx
    block_id = ctx_id * n_exp + exp_id
    base_row = block_id * tok_dev
    count_below = jnp.sum((expert_picks < base_row).astype(jnp.int32), axis=1)
    inside = jnp.sum(
        ((expert_picks >= base_row) & (expert_picks < base_row + tok_dev)).astype(jnp.int32), axis=1
    )
    offsets = jnp.arange(slot_count, dtype=jnp.int32)
    slot_spots = jnp.minimum(count_below[:, None] + offsets[None, :], expert_picks.shape[1] - 1)
    is_valid = offsets[None, :] < inside[:, None]
    chosen = jnp.where(
        is_valid, jnp.take_along_axis(expert_picks, slot_spots, axis=1) - base_row, 0
    )
    send_rows = jnp.where(is_valid[..., None], moe_input[chosen], jnp.zeros((), jnp.bfloat16))
    send_grads = jnp.where(is_valid[..., None], out_grad[chosen], jnp.zeros((), jnp.bfloat16))
    got_rows, got_grads = (
        lax.all_to_all(
            send_rows.reshape(n_exp, n_local, slot_count, feat_width),
            "exp",
            split_axis=0,
            concat_axis=0,
            tiled=True,
        ),
        lax.all_to_all(
            send_grads.reshape(n_exp, n_local, slot_count, feat_width),
            "exp",
            split_axis=0,
            concat_axis=0,
            tiled=True,
        ),
    )
    my_picks = lax.dynamic_slice(
        expert_picks, (exp_id * n_local, ctx_id * group_picks), (n_local, group_picks)
    )
    src_exp = my_picks // tok_dev - ctx_id * n_exp
    starts = my_picks // tok_dev * tok_dev
    slot_rank = jnp.arange(group_picks, dtype=jnp.int32)[None, :] - jnp.sum(
        (my_picks[:, None, :] < starts[:, :, None]).astype(jnp.int32), axis=2
    )
    flat_pos = (
        (src_exp * n_local + jnp.arange(n_local, dtype=jnp.int32)[:, None]) * slot_count + slot_rank
    ).reshape(-1)
    mine_rows = jnp.take(got_rows.reshape(-1, feat_width), flat_pos, axis=0).reshape(
        n_local, group_picks, feat_width
    )
    mine_grads = jnp.take(got_grads.reshape(-1, feat_width), flat_pos, axis=0).reshape(
        n_local, group_picks, feat_width
    )
    slot_rows, slot_grads = (
        lax.all_gather(mine_rows, "ctx", axis=1, tiled=True),
        lax.all_gather(mine_grads, "ctx", axis=1, tiled=True),
    )
    gate_rows = lax.dynamic_slice_in_dim(gate_probs, exp_id * n_local, n_local, 0)
    pre_gate = jnp.einsum("kcd,kdf->kcf", slot_rows, w_gate, preferred_element_type=jnp.float32)
    pre_up = jnp.einsum("kcd,kdf->kcf", slot_rows, w_up, preferred_element_type=jnp.float32)
    gated_act, act_slope = activation(pre_gate)
    hidden_full = gated_act * pre_up
    hidden = hidden_full.astype(jnp.bfloat16)
    down_back = jnp.einsum("kcd,kfd->kcf", slot_grads, w_down, preferred_element_type=jnp.float32)
    gate_part = settle(jnp.sum(down_back * hidden_full, axis=2))
    scaled = gate_rows[..., None] * down_back
    d_gate = (scaled * pre_up * act_slope).astype(jnp.bfloat16)
    d_up = (scaled * gated_act).astype(jnp.bfloat16)
    weighted = (gate_rows[..., None] * slot_grads.astype(jnp.float32)).astype(jnp.bfloat16)
    dw_down = jnp.einsum(
        "kcf,kcd->kfd", hidden, weighted, preferred_element_type=jnp.float32
    ).astype(jnp.bfloat16)
    dw_gate = jnp.einsum(
        "kcd,kcf->kdf", slot_rows, d_gate, preferred_element_type=jnp.float32
    ).astype(jnp.bfloat16)
    dw_up = jnp.einsum("kcd,kcf->kdf", slot_rows, d_up, preferred_element_type=jnp.float32).astype(
        jnp.bfloat16
    )
    dx_part = settle(
        jnp.einsum("kcf,kdf->kcd", d_gate, w_gate, preferred_element_type=jnp.float32)
        + jnp.einsum("kcf,kdf->kcd", d_up, w_up, preferred_element_type=jnp.float32)
    )
    dx_sum, d_gates = (
        lax.psum_scatter(
            dx_part.astype(jnp.bfloat16), "ctx", scatter_dimension=1, tiled=True
        ).astype(jnp.float32),
        lax.psum_scatter(
            gate_part.astype(jnp.bfloat16), "ctx", scatter_dimension=1, tiled=True
        ).astype(jnp.float32),
    )
    dx_slot = dx_sum.astype(jnp.bfloat16)
    back_rows = (
        jnp.zeros((n_exp * n_local * slot_count, feat_width), jnp.bfloat16)
        .at[flat_pos]
        .set(dx_slot.reshape(-1, feat_width))
    )
    returned = lax.all_to_all(
        back_rows.reshape(n_exp, n_local, slot_count, feat_width),
        "exp",
        split_axis=0,
        concat_axis=0,
        tiled=True,
    )
    returned = returned.reshape(-1, feat_width)
    onehot = (
        (chosen.reshape(-1)[None, :] == jnp.arange(tok_dev, dtype=jnp.int32)[:, None])
        & is_valid.reshape(-1)[None, :]
    ).astype(jnp.bfloat16)
    d_resid = (
        out_grad.astype(jnp.float32) + jnp.dot(onehot, returned, preferred_element_type=jnp.float32)
    ).astype(jnp.bfloat16)
    tok_ctx, head_dim = queries.shape
    key_scale = head_dim ** (-0.5)
    piece_rows = lax.all_gather(d_resid, "exp", axis=0, tiled=True)
    out_rows = contract_last(piece_rows, w_out)
    d_out_acc = out_rows.astype(jnp.bfloat16)
    dw_part = contract_first(attn_out, piece_rows)
    d_out, dw_part = (d_out_acc, dw_part)
    dw_out = lax.psum_scatter(
        settle(dw_part).astype(jnp.bfloat16), "ctx", scatter_dimension=1, tiled=True
    )
    row_delta = jnp.sum(d_out.astype(jnp.float32) * attn_out.astype(jnp.float32), axis=1)
    lse_all = log_norm[0]
    keys_here, values_here = (attn_keys, values)
    key_pos = ctx_id * tok_ctx + jnp.arange(tok_ctx, dtype=jnp.int32)
    key_pieces = 1
    delta_all = lax.all_gather(row_delta, "ctx", axis=0, tiled=True)
    q_rows = lax.all_gather(queries, "ctx", axis=0, tiled=True)
    do_rows = lax.all_gather(d_out, "ctx", axis=0, tiled=True)
    add_q, add_k, add_v = tile_grads(
        q_rows, do_rows, lse_all, delta_all, keys_here, values_here, key_pos, key_scale, key_pieces
    )
    dq_all = add_q
    dq_all, grad_keys, grad_values = (dq_all, add_k, add_v)
    grad_q = lax.psum_scatter(dq_all.astype(jnp.bfloat16), "ctx", scatter_dimension=0, tiled=True)
    grad_k = grad_keys.astype(jnp.bfloat16)
    grad_v = grad_values.astype(jnp.bfloat16)
    return (d_resid, dw_gate, dw_up, dw_down, d_gates, dw_out, grad_q, grad_k, grad_v)


def solution(mesh):
    return jax.shard_map(
        body,
        mesh=mesh,
        in_specs=(
            P(("ctx", "exp"), None),
            P(("ctx", "exp"), None),
            P("exp", None, "ctx"),
            P("exp", None, "ctx"),
            P("exp", "ctx", None),
            P(),
            P(),
            P("ctx", "exp"),
            P("ctx", "exp"),
            P("ctx", "exp"),
            P("ctx", "exp"),
            P("exp", None),
            P("exp", None),
        ),
        out_specs=(
            P(("ctx", "exp"), None),
            P("exp", None, "ctx"),
            P("exp", None, "ctx"),
            P("exp", "ctx", None),
            P("exp", "ctx"),
            P("exp", "ctx"),
            P("ctx", "exp"),
            P("ctx", "exp"),
            P("ctx", "exp"),
        ),
        check_vma=False,
    )
```

profile of v0, /device:TPU:0, one launch (start us, length us, event | category | flops | bytes accessed | tf_op | source)
XLA Modules:
  0.0 887.2 jit_solution(8527836403347974611)
XLA Ops:
  20.6 5.5 all-to-all-start
  26.4 10.5 %all-to-all-done = bf16[16,2,2,4096]{3,2,1,0:T(2,128)(2,1)S(1)} async-done(((bf16[16,2,2,4096]{3,2,1,0:T(2,128)(2,1)}), bf16[16,2,2,4096]{3,2,1,0:T(2,128)(2,1)S(1)}, u32[]{:S(2)}, u32[]{:S(2)}) %all-to-all-start) | async-done | bytes 524320 | tf_op jit(solution)/shard_map/all_to_all | solution.py:136
  36.9 4.2 all-to-all-start.1
  44.0 8.1 all-to-all-done.1
  58.2 52.4 %all-gather.8.cloned.1.call-done = bf16[2,128,4096]{2,1,0:T(8,128)(2,1)} async-done(((bf16[2,16,4096]{2,1,0:T(8,128)(2,1)}), bf16[2,128,4096]{2,1,0:T(8,128)(2,1)}) %all-gather.8.cloned.1.call-update) | async-done | bytes 2097168 | tf_op jit(solution)/shard_map/all_gather | solution.py:162
  114.6 50.8 %all-gather.6.cloned.1.call-done = bf16[2,128,4096]{2,1,0:T(8,128)(2,1)} async-done(((bf16[2,16,4096]{2,1,0:T(8,128)(2,1)}), bf16[2,128,4096]{2,1,0:T(8,128)(2,1)}) %all-gather.6.cloned.1.call-update) | async-done | bytes 2097168 | tf_op jit(solution)/shard_map/all_gather | solution.py:163
  172.9 73.0 %reduce-scatter.7.cloned.1.call-done = bf16[2,16,4096]{2,1,0:T(8,128)(2,1)} async-done(((bf16[2,128,4096]{2,1,0:T(8,128)(2,1)}), bf16[2,16,4096]{2,1,0:T(8,128)(2,1)}) %reduce-scatter.7.cloned.1.call-update) | async-done | bytes 262160 | tf_op jit(solution)/shard_map/reduce_scatter | solution.py:191
  248.6 4.4 all-to-all-start.2
  253.9 9.9 %all-to-all-done.2 = bf16[16,2,2,4096]{3,2,1,0:T(2,128)(2,1)S(1)} async-done(((bf16[16,2,2,4096]{3,2,1,0:T(2,128)(2,1)}), bf16[16,2,2,4096]{3,2,1,0:T(2,128)(2,1)S(1)}, u32[]{:S(2)}, u32[]{:S(2)}) %all-to-all-start.2) | async-done | bytes 524320 | tf_op jit(solution)/shard_map/all_to_all | solution.py:204
  265.7 88.6 %all-gather.10.cloned.1.call-done = bf16[2048,4096]{1,0:T(8,128)(2,1)} async-done(((bf16[128,4096]{1,0:T(8,128)(2,1)}), bf16[2048,4096]{1,0:T(8,128)(2,1)}) %all-gather.10.cloned.1.call-update) | async-done | bytes 16777232 | tf_op jit(solution)/shard_map/all_gather | solution.py:221
  354.4 12.4 %multiply_reduce_fusion = (f32[2048]{0:T(1024)S(1)}, bf16[2048,128]{0,1:T(8,128)(2,1)}) fusion(bf16[2048,128]{0,1:T(8,128)(2,1)S(1)} %copy.31, bf16[2048,4096]{1,0:T(8,128)(2,1)} %all-gather.10.cloned.1.call-done, bf16[128,4096]{1,0:T(8,128)(2,1)} %param.31), kind=kOutput, calls=%fused_computation.41 | convolution fusion | flops 2148792320 | bytes 18882560 | tf_op jit(solution)/shard_map/dot_general | solution.py:26
  368.9 9.2 %fusion.18 = bf16[128,4096]{0,1:T(8,128)(2,1)} fusion(bf16[2048,4096]{1,0:T(8,128)(2,1)} %all-gather.10.cloned.1.call-done, bf16[2048,128]{1,0:T(8,128)(2,1)S(1)} %copy-done.16), kind=kOutput, calls=%fused_computation.37 | convolution fusion | flops 2148007936 | bytes 18350080 | tf_op jit(solution)/shard_map/dot_general | solution.py:20
  378.1 36.5 %all_gather.23 = f32[16384]{0:T(1024)} all-gather(f32[2048]{0:T(1024)S(1)} %get-tuple-element.634), channel_id=1, replica_groups=mesh['ctx'=8,'exp'=16] {'ctx'}, dimensions={0}, use_global_device_ids=true | all-gather | bytes 73728 | tf_op jit(solution)/shard_map/all_gather | solution.py:234
  414.7 24.9 %all-gather.14.cloned.1.call-done = bf16[16384,128]{0,1:T(8,128)(2,1)} async-done(((bf16[2048,128]{0,1:T(8,128)(2,1)}), bf16[16384,128]{0,1:T(8,128)(2,1)}) %all-gather.14.cloned.1.call-update) | async-done | bytes 4194320 | tf_op jit(solution)/shard_map/all_gather | solution.py:236
  439.6 6.4 copy.32
  446.0 65.2 %all-gather.12.cloned.1.call-done = bf16[16384,128]{1,0:T(8,128)(2,1)} async-done(((bf16[2048,128]{1,0:T(8,128)(2,1)}), bf16[16384,128]{1,0:T(8,128)(2,1)}) %all-gather.12.cloned.1.call-update) | async-done | bytes 4194320 | tf_op jit(solution)/shard_map/all_gather | solution.py:235
  513.4 285.8 %while.22 = (s32[]{:T(128)}, bf16[16384,128]{1,0:T(8,128)(2,1)}, f32[2048,128]{1,0:T(8,128)}, f32[2048,128]{1,0:T(8,128)}, s32[]{:T(128)}, /*index=5*/bf16[16384...) while((s32[]{:T(128)}, bf16[16384,128]{1,0:T(8,128)(2,1)}, ...), condition=%wide.region_13.15_spmd.clone, body=%wide.region_10.14_spmd.clone.sunk | while | flops 5420617728 | bytes 126487464 | solution.py:88
  524.2 28.8 %conditional.3 = (f32[2048,128]{1,0:T(8,128)}, f32[2048,128]{1,0:T(8,128)S(1)}, f32[2048,128]{1,0:T(8,128)S(1)}) conditional(s32[]{:T(128)} %convert_element_type.156, () %tuple.94, (s32[]{:T(128)}, s32[]{:T(128)}, s32[2048]{0:T(1024)S(1)}, bf16[16384,128]{1,0:T(8,128)(2,1)}, s32[]{:T(128)}, /*index=5*/bf16[2048,128]{1,0:T(8,128)(2,1)S(1)}, ...), branch_computations={%region_11.12_spmd, %region_12.13_spmd} | conditional | flops 5419569152 | bytes 118089824 | solution.py:73
  525.7 3.4 fusion.8
  529.1 6.2 fusion.3
  535.2 8.3 multiply_convert_fusion
  543.6 6.0 convolution_multiply_fusion
  557.4 28.7 %conditional.3 = (f32[2048,128]{1,0:T(8,128)}, f32[2048,128]{1,0:T(8,128)S(1)}, f32[2048,128]{1,0:T(8,128)S(1)}) conditional(s32[]{:T(128)} %convert_element_type.156, () %tuple.94, (s32[]{:T(128)}, s32[]{:T(128)}, s32[2048]{0:T(1024)S(1)}, bf16[16384,128]{1,0:T(8,128)(2,1)}, s32[]{:T(128)}, /*index=5*/bf16[2048,128]{1,0:T(8,128)(2,1)S(1)}, ...), branch_computations={%region_11.12_spmd, %region_12.13_spmd} | conditional | flops 5419569152 | bytes 118089824 | solution.py:73
  558.8 3.4 fusion.8
  562.2 6.2 fusion.3
  568.4 8.3 multiply_convert_fusion
  576.7 6.0 convolution_multiply_fusion
  582.7 3.4 convolution_multiply_fusion.1
  592.0 28.8 %conditional.3 = (f32[2048,128]{1,0:T(8,128)}, f32[2048,128]{1,0:T(8,128)S(1)}, f32[2048,128]{1,0:T(8,128)S(1)}) conditional(s32[]{:T(128)} %convert_element_type.156, () %tuple.94, (s32[]{:T(128)}, s32[]{:T(128)}, s32[2048]{0:T(1024)S(1)}, bf16[16384,128]{1,0:T(8,128)(2,1)}, s32[]{:T(128)}, /*index=5*/bf16[2048,128]{1,0:T(8,128)(2,1)S(1)}, ...), branch_computations={%region_11.12_spmd, %region_12.13_spmd} | conditional | flops 5419569152 | bytes 118089824 | solution.py:73
  593.5 3.4 fusion.8
  596.9 6.2 fusion.3
  603.0 8.3 multiply_convert_fusion
  611.4 6.0 convolution_multiply_fusion
  626.7 28.8 %conditional.3 = (f32[2048,128]{1,0:T(8,128)}, f32[2048,128]{1,0:T(8,128)S(1)}, f32[2048,128]{1,0:T(8,128)S(1)}) conditional(s32[]{:T(128)} %convert_element_type.156, () %tuple.94, (s32[]{:T(128)}, s32[]{:T(128)}, s32[2048]{0:T(1024)S(1)}, bf16[16384,128]{1,0:T(8,128)(2,1)}, s32[]{:T(128)}, /*index=5*/bf16[2048,128]{1,0:T(8,128)(2,1)S(1)}, ...), branch_computations={%region_11.12_spmd, %region_12.13_spmd} | conditional | flops 5419569152 | bytes 118089824 | solution.py:73
  628.1 3.4 fusion.8
  631.6 6.2 fusion.3
  637.7 8.3 multiply_convert_fusion
  646.1 6.0 convolution_multiply_fusion
  652.1 3.4 convolution_multiply_fusion.1
  661.4 28.7 %conditional.3 = (f32[2048,128]{1,0:T(8,128)}, f32[2048,128]{1,0:T(8,128)S(1)}, f32[2048,128]{1,0:T(8,128)S(1)}) conditional(s32[]{:T(128)} %convert_element_type.156, () %tuple.94, (s32[]{:T(128)}, s32[]{:T(128)}, s32[2048]{0:T(1024)S(1)}, bf16[16384,128]{1,0:T(8,128)(2,1)}, s32[]{:T(128)}, /*index=5*/bf16[2048,128]{1,0:T(8,128)(2,1)S(1)}, ...), branch_computations={%region_11.12_spmd, %region_12.13_spmd} | conditional | flops 5419569152 | bytes 118089824 | solution.py:73
  662.8 3.4 fusion.8
  666.2 6.2 fusion.3
  672.4 8.3 multiply_convert_fusion
  680.7 6.0 convolution_multiply_fusion
  686.7 3.4 convolution_multiply_fusion.1
  696.0 28.7 %conditional.3 = (f32[2048,128]{1,0:T(8,128)}, f32[2048,128]{1,0:T(8,128)S(1)}, f32[2048,128]{1,0:T(8,128)S(1)}) conditional(s32[]{:T(128)} %convert_element_type.156, () %tuple.94, (s32[]{:T(128)}, s32[]{:T(128)}, s32[2048]{0:T(1024)S(1)}, bf16[16384,128]{1,0:T(8,128)(2,1)}, s32[]{:T(128)}, /*index=5*/bf16[2048,128]{1,0:T(8,128)(2,1)S(1)}, ...), branch_computations={%region_11.12_spmd, %region_12.13_spmd} | conditional | flops 5419569152 | bytes 118089824 | solution.py:73
  697.4 3.4 fusion.8
  700.8 6.2 fusion.3
  707.0 8.3 multiply_convert_fusion
  715.3 6.0 convolution_multiply_fusion
  721.3 3.4 convolution_multiply_fusion.1
  730.6 28.7 %conditional.3 = (f32[2048,128]{1,0:T(8,128)}, f32[2048,128]{1,0:T(8,128)S(1)}, f32[2048,128]{1,0:T(8,128)S(1)}) conditional(s32[]{:T(128)} %convert_element_type.156, () %tuple.94, (s32[]{:T(128)}, s32[]{:T(128)}, s32[2048]{0:T(1024)S(1)}, bf16[16384,128]{1,0:T(8,128)(2,1)}, s32[]{:T(128)}, /*index=5*/bf16[2048,128]{1,0:T(8,128)(2,1)S(1)}, ...), branch_computations={%region_11.12_spmd, %region_12.13_spmd} | conditional | flops 5419569152 | bytes 118089824 | solution.py:73
  732.0 3.4 fusion.8
  735.4 6.2 fusion.3
  741.6 8.3 multiply_convert_fusion
  750.0 6.0 convolution_multiply_fusion
  756.0 3.4 convolution_multiply_fusion.1
  765.2 28.7 %conditional.3 = (f32[2048,128]{1,0:T(8,128)}, f32[2048,128]{1,0:T(8,128)S(1)}, f32[2048,128]{1,0:T(8,128)S(1)}) conditional(s32[]{:T(128)} %convert_element_type.156, () %tuple.94, (s32[]{:T(128)}, s32[]{:T(128)}, s32[2048]{0:T(1024)S(1)}, bf16[16384,128]{1,0:T(8,128)(2,1)}, s32[]{:T(128)}, /*index=5*/bf16[2048,128]{1,0:T(8,128)(2,1)S(1)}, ...), branch_computations={%region_11.12_spmd, %region_12.13_spmd} | conditional | flops 5419569152 | bytes 118089824 | solution.py:73
  766.6 3.4 fusion.8
  770.0 6.2 fusion.3
  776.2 8.3 multiply_convert_fusion
  784.6 6.0 convolution_multiply_fusion
  790.6 3.4 convolution_multiply_fusion.1
  815.5 64.9 %reduce-scatter.11.cloned.1.call-done = bf16[2048,128]{1,0:T(8,128)(2,1)} async-done(((bf16[16384,128]{1,0:T(8,128)(2,1)}), bf16[2048,128]{1,0:T(8,128)(2,1)}) %reduce-scatter.11.cloned.1.call-update) | async-done | bytes 524304 | tf_op jit(solution)/shard_map/reduce_scatter | solution.py:242
  (208 shorter events, 118.6 us)
Async XLA Ops:
  7.2 103.4 %copy-start = (bf16[2,4096,176]{1,2,0:T(8,128)(2,1)S(1)}, bf16[2,4096,176]{1,2,0:T(8,128)(2,1)}, u32[]{:S(2)}) copy-start(bf16[2,4096,176]{1,2,0:T(8,128)(2,1)} %param.21) | copy-start | bytes 8650756
  7.2 1.4 copy-start.2
  20.6 16.4 %all-to-all-start = ((bf16[16,2,2,4096]{3,2,1,0:T(2,128)(2,1)}), bf16[16,2,2,4096]{3,2,1,0:T(2,128)(2,1)S(1)}, u32[]{:S(2)}, u32[]{:S(2)}) async-start(bf16[16,2,2,4096]{3,2,1,0:T(2,128)(2,1)} %get-tuple-element.630), calls=%async_computation | async-start | bytes 1048576 | tf_op jit(solution)/shard_map/all_to_all | solution.py:136
  36.9 4.3 copy-start.11
  36.9 15.1 %all-to-all-start.1 = ((bf16[16,2,2,4096]{3,2,1,0:T(2,128)(2,1)}), bf16[16,2,2,4096]{3,2,1,0:T(2,128)(2,1)}, u32[]{:S(2)}, u32[]{:S(2)}) async-start(bf16[16,2,2,4096]{3,2,1,0:T(2,128)(2,1)} %get-tuple-element.631), calls=%async_computation.1 | async-start | bytes 1048576 | tf_op jit(solution)/shard_map/all_to_all | solution.py:129
  41.2 69.4 %all-gather.8.cloned.1.call-start = ((), (), s32[]{:S(2)}) async-start(), calls=%async_computation.8 | async-start | bytes 2359296 | tf_op jit(solution)/shard_map/all_gather | solution.py:162
  56.7 108.7 %all-gather.6.cloned.1.call-start = ((), (), s32[]{:S(2)}) async-start(), calls=%async_computation.7 | async-start | bytes 2359296 | tf_op jit(solution)/shard_map/all_gather | solution.py:163
  57.4 188.5 %reduce-scatter.7.cloned.1.call-start = ((), (), s32[]{:S(2)}) async-start(), calls=%async_computation.9 | async-start | bytes 2359296 | tf_op jit(solution)/shard_map/reduce_scatter | solution.py:191
  58.2 107.2 %copy-start.21 = (f32[2,128]{1,0:T(2,128)}, f32[2,128]{1,0:T(2,128)S(1)}, u32[]{:S(2)}) copy-start(f32[2,128]{1,0:T(2,128)S(1)} %constant_dynamic-slice_fusion) | copy-start | bytes 3076
  110.6 2.7 copy-start.3
  110.6 3.1 copy-start.8
  113.7 55.1 %copy-start.12 = (f32[2,128,176]{1,2,0:T(8,128)}, f32[2,128,176]{1,2,0:T(8,128)S(1)}, u32[]{:S(2)}) copy-start(f32[2,128,176]{1,2,0:T(8,128)S(1)} %fusion.35) | copy-start | bytes 540676
  114.6 55.0 %copy-start.14 = (f32[2,128,176]{1,2,0:T(8,128)}, f32[2,128,176]{1,2,0:T(8,128)S(1)}, u32[]{:S(2)}) copy-start(f32[2,128,176]{1,2,0:T(8,128)S(1)} %fusion.34) | copy-start | bytes 540676
  168.8 4.0 copy-start.17
  168.8 4.0 copy-start.19
  168.8 1.9 copy-start.9
  172.8 91.2 %copy-start.6 = (bf16[128,4096]{1,0:T(8,128)(2,1)S(1)}, bf16[128,4096]{1,0:T(8,128)(2,1)}, u32[]{:S(2)}) copy-start(bf16[128,4096]{1,0:T(8,128)(2,1)} %param.20) | copy-start | bytes 3145732
  172.8 92.7 %copy-start.16 = (bf16[2048,128]{1,0:T(8,128)(2,1)S(1)}, bf16[2048,128]{1,0:T(8,128)(2,1)}, u32[]{:S(2)}) copy-start(bf16[2048,128]{1,0:T(8,128)(2,1)} %param.29) | copy-start | bytes 1572868
  248.6 15.2 %all-to-all-start.2 = ((bf16[16,2,2,4096]{3,2,1,0:T(2,128)(2,1)}), bf16[16,2,2,4096]{3,2,1,0:T(2,128)(2,1)S(1)}, u32[]{:S(2)}, u32[]{:S(2)}) async-start(bf16[16,2,2,4096]{3,2,1,0:T(2,128)(2,1)} %reshape.304), calls=%async_computation.3 | async-start | bytes 1048576 | tf_op jit(solution)/shard_map/all_to_all | solution.py:204
  253.0 101.4 %all-gather.10.cloned.1.call-start = ((), (), s32[]{:S(2)}) async-start(), calls=%async_computation.10 | async-start | bytes 17825792 | tf_op jit(solution)/shard_map/all_gather | solution.py:221
  265.5 174.1 %all-gather.14.cloned.1.call-start = ((), (), s32[]{:S(2)}) async-start(), calls=%async_computation.13 | async-start | bytes 4718592 | tf_op jit(solution)/shard_map/all_gather | solution.py:236
  366.8 144.3 %all-gather.12.cloned.1.call-start = ((), (), s32[]{:S(2)}) async-start(), calls=%async_computation.12 | async-start | bytes 4718592 | tf_op jit(solution)/shard_map/all_gather | solution.py:235
  367.4 441.0 %reduce-scatter.13.cloned.1.call-start = ((), (), s32[]{:S(2)}) async-start(), calls=%async_computation.15 | async-start | bytes 36864
  368.9 440.8 %reduce-scatter.9.cloned.1.call-start = ((), (), s32[]{:S(2)}) async-start(), calls=%async_computation.11 | async-start | bytes 1179648 | tf_op jit(solution)/shard_map/reduce_scatter | solution.py:226
  414.6 465.8 %reduce-scatter.11.cloned.1.call-start = ((), (), s32[]{:S(2)}) async-start(), calls=%async_computation.14 | async-start | bytes 4718592 | tf_op jit(solution)/shard_map/reduce_scatter | solution.py:242
  446.0 67.4 %copy-start.7 = (bf16[2048,128]{1,0:T(8,128)(2,1)S(1)}, bf16[2048,128]{1,0:T(8,128)(2,1)}, u32[]{:S(2)}) copy-start(bf16[2048,128]{1,0:T(8,128)(2,1)} %param.27) | copy-start | bytes 1572868
  529.0 6.2 copy-start.23
  543.6 6.0 copy-start.24
  562.2 6.2 copy-start.23
  576.7 6.0 copy-start.24
  596.9 6.2 copy-start.23
  611.4 6.0 copy-start.24
  631.5 6.2 copy-start.23
  646.1 6.1 copy-start.24
  666.2 6.2 copy-start.23
  680.7 6.0 copy-start.24
  700.8 6.2 copy-start.23
  715.3 6.0 copy-start.24
  735.4 6.2 copy-start.23
  749.9 6.0 copy-start.24
  770.0 6.2 copy-start.23
  784.5 6.0 copy-start.24
  799.2 1.6 copy-start.4
  799.2 1.6 copy-start.20
  799.2 4.1 copy-start.18
  800.8 2.5 copy-start.5
  800.8 5.0 copy-start.10
  800.8 5.0 copy-start.13
  800.8 5.0 copy-start.15
  800.8 5.0 copy-start.22
  803.3 77.2 %copy-start.1 = (bf16[2,4096,176]{1,2,0:T(8,128)(2,1)S(1)}, bf16[2,4096,176]{1,2,0:T(8,128)(2,1)}, u32[]{:S(2)}) copy-start(bf16[2,4096,176]{1,2,0:T(8,128)(2,1)} %param.21) | copy-start | bytes 8650756
Sparse Core Ops, SparseCore 0:
  56.8 53.7 all-gather.7
  113.5 51.8 all-gather.5
  172.9 72.9 reduce-scatter.6
  265.6 88.7 all-gather.9
  366.9 72.5 all-gather.13
  441.8 69.3 all-gather.11
  514.5 59.8 reduce-scatter.12
  578.0 70.7 reduce-scatter.8
  799.3 81.0 reduce-scatter.10
where the time goes:
time: 898 us; the launch traced here: 887 us
  waiting for transfers between devices  450 us (50%)
  matrix products  258 us (29%)
  local copies, waits for them, and re-layouts  61.6 us (7%)
  blocking collectives  36.5 us (4%)
  other arithmetic  35.8 us (4%)
  loops' own time  15.8 us (2%)
  starting transfers between devices  14.9 us (2%)
  between operations  14.5 us (2%)
    dot_general x17, matrix products, contract_first(): lax.dot_general(left, right, (((0,), (0,)), ((), ())), preferred_element_...  107 us
    dot_general x17, matrix products, contract_last(): lax.dot_general(left, right, (((1,), (1,)), ((), ())), preferred_element_...  106 us
    all_gather x1, waiting for transfers between devices, body(): piece_rows = lax.all_gather(d_resid, 'exp', axis=0, tiled=True)  88.6 us
    reduce_scatter x1, waiting for transfers between devices, body(): lax.psum_scatter(dx_part.astype(jnp.bfloat16), 'ctx', scatter_dimension=1...  73 us
    all_gather x1, waiting for transfers between devices, body(): q_rows = lax.all_gather(queries, 'ctx', axis=0, tiled=True)  65.2 us
    reduce_scatter x1, waiting for transfers between devices, body(): lax.psum_scatter(dq_all.astype(jnp.bfloat16), 'ctx', scatter_dimension=0,...  64.9 us
    all_gather x1, waiting for transfers between devices, body(): lax.all_gather(mine_rows, 'ctx', axis=1, tiled=True)  52.4 us
    all_gather x1, waiting for transfers between devices, body(): lax.all_gather(mine_grads, 'ctx', axis=1, tiled=True)  50.8 us
  transfers between devices with their start and end apart: 12, of which 10 were waited for; matrix products, arithmetic and copies ran while one was open for 35% of the time, Pallas kernels for 0%

commit v1 on v0

--- a/solution.py
+++ b/solution.py
@@ -218,7 +218,9 @@
     ).astype(jnp.bfloat16)
     tok_ctx, head_dim = queries.shape
     key_scale = head_dim ** (-0.5)
-    piece_rows = lax.all_gather(d_resid, "exp", axis=0, tiled=True)
+    piece_rows = jnp.concatenate(
+        lax.all_to_all(jnp.stack([d_resid] * lax.axis_size("exp")), "exp", 0, 0), axis=0
+    )
     out_rows = contract_last(piece_rows, w_out)
     d_out_acc = out_rows.astype(jnp.bfloat16)
     dw_part = contract_first(attn_out, piece_rows)

time: 898 us -> 1050 us (1.17)
  waiting for transfers between devices: 450 us -> 584 us
    all_to_all x0 -> x1, waiting for transfers between devices: none -> 224 us  [body(): lax.all_to_all(jnp.stack([d_resid] * lax.axis_size('exp')), 'exp', 0, 0)]
    all_gather x1 -> x0, waiting for transfers between devices: 88.6 us -> none  [body(): piece_rows = lax.all_gather(d_resid, 'exp', axis=0, tiled=True)]
    dot_general x8, matrix products: 27 us -> 54.9 us  [compute_tile(): jnp.dot(d_scores, keys_piece, preferred_element_type=jnp.float32)]
    dot_general x17, matrix products: 107 us -> 85.9 us  [contract_first(): lax.dot_general(left, right, (((0,), (0,)), ((), ())), preferred_element_...]
  transfers between devices with their start and end apart: 12 -> 12, of which waited for: 10 -> 10; matrix products, arithmetic and copies ran while one was open for 35% -> 31% of each run, Pallas kernels for 0% -> 0%
where the time goes in v1:
time: 1050 us; the launch traced here: 1040 us
  waiting for transfers between devices  584 us (56%)
  matrix products  266 us (25%)
  local copies, waits for them, and re-layouts  68 us (6%)
  blocking collectives  35.7 us (3%)
  other arithmetic  35.6 us (3%)
  starting transfers between devices  20.1 us (2%)
  loops' own time  15.3 us (1%)
  between operations  14.8 us (1%)
    all_to_all x1, waiting for transfers between devices, body(): lax.all_to_all(jnp.stack([d_resid] * lax.axis_size('exp')), 'exp', 0, 0)  224 us
    dot_general x17, matrix products, contract_last(): lax.dot_general(left, right, (((1,), (1,)), ((), ())), preferred_element_...  107 us
    dot_general x17, matrix products, contract_first(): lax.dot_general(left, right, (((0,), (0,)), ((), ())), preferred_element_...  85.9 us
    reduce_scatter x1, waiting for transfers between devices, body(): lax.psum_scatter(dx_part.astype(jnp.bfloat16), 'ctx', scatter_dimension=1...  73 us
    all_gather x1, waiting for transfers between devices, body(): q_rows = lax.all_gather(queries, 'ctx', axis=0, tiled=True)  65.2 us
    reduce_scatter x1, waiting for transfers between devices, body(): lax.psum_scatter(dq_all.astype(jnp.bfloat16), 'ctx', scatter_dimension=0,...  64.8 us
    dot_general x8, matrix products, compute_tile(): jnp.dot(d_scores, keys_piece, preferred_element_type=jnp.float32)  54.9 us
    all_gather x1, waiting for transfers between devices, body(): lax.all_gather(mine_rows, 'ctx', axis=1, tiled=True)  52.4 us
  transfers between devices with their start and end apart: 12, of which 10 were waited for; matrix products, arithmetic and copies ran while one was open for 31% of the time, Pallas kernels for 0%

profile of v1, /device:TPU:0, one launch (start us, length us, event | category | flops | bytes accessed | tf_op | source)
XLA Modules:
  0.0 1040.1 jit_solution(9660725704020494511)
XLA Ops:
  20.6 5.5 all-to-all-start
  26.4 10.5 %all-to-all-done = bf16[16,2,2,4096]{3,2,1,0:T(2,128)(2,1)S(1)} async-done(((bf16[16,2,2,4096]{3,2,1,0:T(2,128)(2,1)}), bf16[16,2,2,4096]{3,2,1,0:T(2,128)(2,1)S(1)}, u32[]{:S(2)}, u32[]{:S(2)}) %all-to-all-start) | async-done | bytes 524320 | tf_op jit(solution)/shard_map/all_to_all | solution.py:136
  36.9 4.2 all-to-all-start.1
  43.9 8.1 all-to-all-done.1
  58.2 52.4 %all-gather.7.cloned.1.call-done = bf16[2,128,4096]{2,1,0:T(8,128)(2,1)} async-done(((bf16[2,16,4096]{2,1,0:T(8,128)(2,1)}), bf16[2,128,4096]{2,1,0:T(8,128)(2,1)}) %all-gather.7.cloned.1.call-update) | async-done | bytes 2097168 | tf_op jit(solution)/shard_map/all_gather | solution.py:162
  110.6 3.5 fusion.34
  115.1 50.3 %all-gather.5.cloned.1.call-done = bf16[2,128,4096]{2,1,0:T(8,128)(2,1)} async-done(((bf16[2,16,4096]{2,1,0:T(8,128)(2,1)}), bf16[2,128,4096]{2,1,0:T(8,128)(2,1)}) %all-gather.5.cloned.1.call-update) | async-done | bytes 2097168 | tf_op jit(solution)/shard_map/all_gather | solution.py:163
  172.9 73.0 %reduce-scatter.7.cloned.1.call-done = bf16[2,16,4096]{2,1,0:T(8,128)(2,1)} async-done(((bf16[2,128,4096]{2,1,0:T(8,128)(2,1)}), bf16[2,16,4096]{2,1,0:T(8,128)(2,1)}) %reduce-scatter.7.cloned.1.call-update) | async-done | bytes 262160 | tf_op jit(solution)/shard_map/reduce_scatter | solution.py:191
  248.6 4.8 all-to-all-start.2
  253.8 10.4 all-to-all-done.2
  265.8 5.9 stack.2
  271.7 5.3 all-to-all-start.3
  277.3 224.4 %all-to-all-done.3 = bf16[16,128,4096]{2,1,0:T(8,128)(2,1)} async-done(((bf16[16,128,4096]{2,1,0:T(8,128)(2,1)}), bf16[16,128,4096]{2,1,0:T(8,128)(2,1)}, u32[]{:S(2)}, u32[]{:S(2)}) %all-to-all-start.3) | async-done | bytes 16777248 | tf_op jit(solution)/shard_map/all_to_all | solution.py:222
  501.7 12.2 %multiply_reduce_fusion = (f32[2048]{0:T(1024)S(1)}, bf16[2048,128]{0,1:T(8,128)(2,1)}) fusion(bf16[2048,128]{0,1:T(8,128)(2,1)S(1)} %copy.31, bf16[2048,4096]{1,0:T(8,128)(2,1)} %bitcast.4, bf16[128,4096]{1,0:T(8,128)(2,1)S(1)} %copy-done.25), kind=kOutput, calls=%fused_computation.41 | convolution fusion | flops 2148792320 | bytes 18882560 | tf_op jit(solution)/shard_map/dot_general | solution.py:26
  516.0 9.2 fusion.18
  525.2 35.7 %all_gather.19 = f32[16384]{0:T(1024)} all-gather(f32[2048]{0:T(1024)S(1)} %get-tuple-element.634), channel_id=1, replica_groups=mesh['ctx'=8,'exp'=16] {'ctx'}, dimensions={0}, use_global_device_ids=true | all-gather | bytes 73728 | tf_op jit(solution)/shard_map/all_gather | solution.py:236
  561.0 24.0 %all-gather.11.cloned.1.call-done = bf16[16384,128]{0,1:T(8,128)(2,1)} async-done(((bf16[2048,128]{0,1:T(8,128)(2,1)}), bf16[16384,128]{0,1:T(8,128)(2,1)}) %all-gather.11.cloned.1.call-update) | async-done | bytes 4194320 | tf_op jit(solution)/shard_map/all_gather | solution.py:238
  585.1 6.4 copy.32
  591.5 65.2 %all-gather.9.cloned.1.call-done = bf16[16384,128]{1,0:T(8,128)(2,1)} async-done(((bf16[2048,128]{1,0:T(8,128)(2,1)}), bf16[16384,128]{1,0:T(8,128)(2,1)}) %all-gather.9.cloned.1.call-update) | async-done | bytes 4194320 | tf_op jit(solution)/shard_map/all_gather | solution.py:237
  658.8 293.1 %while.22 = (s32[]{:T(128)}, bf16[16384,128]{1,0:T(8,128)(2,1)}, f32[2048,128]{1,0:T(8,128)}, f32[2048,128]{1,0:T(8,128)}, s32[]{:T(128)}, /*index=5*/bf16[16384...) while((s32[]{:T(128)}, bf16[16384,128]{1,0:T(8,128)(2,1)}, ...), condition=%wide.region_13.15_spmd.clone, body=%wide.region_10.14_spmd.clone.sunk | while | flops 5420617728 | bytes 126553064 | solution.py:88
  669.5 29.8 %conditional.3 = (f32[2048,128]{1,0:T(8,128)}, f32[2048,128]{1,0:T(8,128)S(1)}, f32[2048,128]{1,0:T(8,128)S(1)}) conditional(s32[]{:T(128)} %convert_element_type.156, () %tuple.94, (s32[]{:T(128)}, s32[]{:T(128)}, s32[2048]{0:T(1024)S(1)}, bf16[16384,128]{1,0:T(8,128)(2,1)}, s32[]{:T(128)}, /*index=5*/bf16[2048,128]{1,0:T(8,128)(2,1)S(1)}, ...), branch_computations={%region_11.12_spmd, %region_12.13_spmd} | conditional | flops 5419569152 | bytes 118155424 | solution.py:73
  674.4 8.4 multiply_convert_fusion
  682.8 6.9 convolution_multiply_fusion.1
  689.7 3.5 convolution_multiply_fusion
  693.2 6.1 fusion.3
  703.6 29.8 %conditional.3 = (f32[2048,128]{1,0:T(8,128)}, f32[2048,128]{1,0:T(8,128)S(1)}, f32[2048,128]{1,0:T(8,128)S(1)}) conditional(s32[]{:T(128)} %convert_element_type.156, () %tuple.94, (s32[]{:T(128)}, s32[]{:T(128)}, s32[2048]{0:T(1024)S(1)}, bf16[16384,128]{1,0:T(8,128)(2,1)}, s32[]{:T(128)}, /*index=5*/bf16[2048,128]{1,0:T(8,128)(2,1)S(1)}, ...), branch_computations={%region_11.12_spmd, %region_12.13_spmd} | conditional | flops 5419569152 | bytes 118155424 | solution.py:73
  703.6 3.5 fusion.8
  708.5 8.4 multiply_convert_fusion
  716.8 6.9 convolution_multiply_fusion.1
  723.7 3.5 convolution_multiply_fusion
  727.2 6.1 fusion.3
  739.1 29.8 %conditional.3 = (f32[2048,128]{1,0:T(8,128)}, f32[2048,128]{1,0:T(8,128)S(1)}, f32[2048,128]{1,0:T(8,128)S(1)}) conditional(s32[]{:T(128)} %convert_element_type.156, () %tuple.94, (s32[]{:T(128)}, s32[]{:T(128)}, s32[2048]{0:T(1024)S(1)}, bf16[16384,128]{1,0:T(8,128)(2,1)}, s32[]{:T(128)}, /*index=5*/bf16[2048,128]{1,0:T(8,128)(2,1)S(1)}, ...), branch_computations={%region_11.12_spmd, %region_12.13_spmd} | conditional | flops 5419569152 | bytes 118155424 | solution.py:73
  744.0 8.4 multiply_convert_fusion
  752.4 6.9 convolution_multiply_fusion.1
  759.3 3.5 convolution_multiply_fusion
  762.8 6.1 fusion.3
  774.7 29.8 %conditional.3 = (f32[2048,128]{1,0:T(8,128)}, f32[2048,128]{1,0:T(8,128)S(1)}, f32[2048,128]{1,0:T(8,128)S(1)}) conditional(s32[]{:T(128)} %convert_element_type.156, () %tuple.94, (s32[]{:T(128)}, s32[]{:T(128)}, s32[2048]{0:T(1024)S(1)}, bf16[16384,128]{1,0:T(8,128)(2,1)}, s32[]{:T(128)}, /*index=5*/bf16[2048,128]{1,0:T(8,128)(2,1)S(1)}, ...), branch_computations={%region_11.12_spmd, %region_12.13_spmd} | conditional | flops 5419569152 | bytes 118155424 | solution.py:73
  779.6 8.4 multiply_convert_fusion
  788.0 6.9 convolution_multiply_fusion.1
  794.9 3.5 convolution_multiply_fusion
  798.4 6.1 fusion.3
  810.3 29.7 %conditional.3 = (f32[2048,128]{1,0:T(8,128)}, f32[2048,128]{1,0:T(8,128)S(1)}, f32[2048,128]{1,0:T(8,128)S(1)}) conditional(s32[]{:T(128)} %convert_element_type.156, () %tuple.94, (s32[]{:T(128)}, s32[]{:T(128)}, s32[2048]{0:T(1024)S(1)}, bf16[16384,128]{1,0:T(8,128)(2,1)}, s32[]{:T(128)}, /*index=5*/bf16[2048,128]{1,0:T(8,128)(2,1)S(1)}, ...), branch_computations={%region_11.12_spmd, %region_12.13_spmd} | conditional | flops 5419569152 | bytes 118155424 | solution.py:73
  810.3 3.5 fusion.8
  815.2 8.4 multiply_convert_fusion
  823.6 6.9 convolution_multiply_fusion.1
  830.4 3.5 convolution_multiply_fusion
  833.9 6.1 fusion.3
  845.8 29.7 %conditional.3 = (f32[2048,128]{1,0:T(8,128)}, f32[2048,128]{1,0:T(8,128)S(1)}, f32[2048,128]{1,0:T(8,128)S(1)}) conditional(s32[]{:T(128)} %convert_element_type.156, () %tuple.94, (s32[]{:T(128)}, s32[]{:T(128)}, s32[2048]{0:T(1024)S(1)}, bf16[16384,128]{1,0:T(8,128)(2,1)}, s32[]{:T(128)}, /*index=5*/bf16[2048,128]{1,0:T(8,128)(2,1)S(1)}, ...), branch_computations={%region_11.12_spmd, %region_12.13_spmd} | conditional | flops 5419569152 | bytes 118155424 | solution.py:73
  845.9 3.5 fusion.8
  850.7 8.4 multiply_convert_fusion
  859.1 6.9 convolution_multiply_fusion.1
  866.0 3.5 convolution_multiply_fusion
  869.5 6.1 fusion.3
  881.4 29.7 %conditional.3 = (f32[2048,128]{1,0:T(8,128)}, f32[2048,128]{1,0:T(8,128)S(1)}, f32[2048,128]{1,0:T(8,128)S(1)}) conditional(s32[]{:T(128)} %convert_element_type.156, () %tuple.94, (s32[]{:T(128)}, s32[]{:T(128)}, s32[2048]{0:T(1024)S(1)}, bf16[16384,128]{1,0:T(8,128)(2,1)}, s32[]{:T(128)}, /*index=5*/bf16[2048,128]{1,0:T(8,128)(2,1)S(1)}, ...), branch_computations={%region_11.12_spmd, %region_12.13_spmd} | conditional | flops 5419569152 | bytes 118155424 | solution.py:73
  886.3 8.4 multiply_convert_fusion
  894.7 6.9 convolution_multiply_fusion.1
  901.5 3.5 convolution_multiply_fusion
  905.0 6.1 fusion.3
  916.9 29.7 %conditional.3 = (f32[2048,128]{1,0:T(8,128)}, f32[2048,128]{1,0:T(8,128)S(1)}, f32[2048,128]{1,0:T(8,128)S(1)}) conditional(s32[]{:T(128)} %convert_element_type.156, () %tuple.94, (s32[]{:T(128)}, s32[]{:T(128)}, s32[2048]{0:T(1024)S(1)}, bf16[16384,128]{1,0:T(8,128)(2,1)}, s32[]{:T(128)}, /*index=5*/bf16[2048,128]{1,0:T(8,128)(2,1)S(1)}, ...), branch_computations={%region_11.12_spmd, %region_12.13_spmd} | conditional | flops 5419569152 | bytes 118155424 | solution.py:73
  921.8 8.4 multiply_convert_fusion
  930.2 6.9 convolution_multiply_fusion.1
  937.1 3.5 convolution_multiply_fusion
  940.6 6.1 fusion.3
  968.2 64.8 %reduce-scatter.11.cloned.1.call-done = bf16[2048,128]{1,0:T(8,128)(2,1)} async-done(((bf16[16384,128]{1,0:T(8,128)(2,1)}), bf16[2048,128]{1,0:T(8,128)(2,1)}) %reduce-scatter.11.cloned.1.call-update) | async-done | bytes 524304 | tf_op jit(solution)/shard_map/reduce_scatter | solution.py:244
  (242 shorter events, 125.2 us)
Async XLA Ops:
  7.2 107.0 %copy-start = (bf16[2,4096,176]{1,2,0:T(8,128)(2,1)S(1)}, bf16[2,4096,176]{1,2,0:T(8,128)(2,1)}, u32[]{:S(2)}) copy-start(bf16[2,4096,176]{1,2,0:T(8,128)(2,1)} %param.21) | copy-start | bytes 8650756
  20.6 16.4 %all-to-all-start = ((bf16[16,2,2,4096]{3,2,1,0:T(2,128)(2,1)}), bf16[16,2,2,4096]{3,2,1,0:T(2,128)(2,1)S(1)}, u32[]{:S(2)}, u32[]{:S(2)}) async-start(bf16[16,2,2,4096]{3,2,1,0:T(2,128)(2,1)} %get-tuple-element.630), calls=%async_computation | async-start | bytes 1048576 | tf_op jit(solution)/shard_map/all_to_all | solution.py:136
  36.9 4.3 copy-start.11
  36.9 15.1 %all-to-all-start.1 = ((bf16[16,2,2,4096]{3,2,1,0:T(2,128)(2,1)}), bf16[16,2,2,4096]{3,2,1,0:T(2,128)(2,1)}, u32[]{:S(2)}, u32[]{:S(2)}) async-start(bf16[16,2,2,4096]{3,2,1,0:T(2,128)(2,1)} %get-tuple-element.631), calls=%async_computation.1 | async-start | bytes 1048576 | tf_op jit(solution)/shard_map/all_to_all | solution.py:129
  41.2 69.4 %all-gather.7.cloned.1.call-start = ((), (), s32[]{:S(2)}) async-start(), calls=%async_computation.9 | async-start | bytes 2359296 | tf_op jit(solution)/shard_map/all_gather | solution.py:162
  56.7 108.7 %all-gather.5.cloned.1.call-start = ((), (), s32[]{:S(2)}) async-start(), calls=%async_computation.8 | async-start | bytes 2359296 | tf_op jit(solution)/shard_map/all_gather | solution.py:163
  57.4 188.5 %reduce-scatter.7.cloned.1.call-start = ((), (), s32[]{:S(2)}) async-start(), calls=%async_computation.10 | async-start | bytes 2359296 | tf_op jit(solution)/shard_map/reduce_scatter | solution.py:191
  58.2 107.2 %copy-start.23 = (f32[2,128]{1,0:T(2,128)}, f32[2,128]{1,0:T(2,128)S(1)}, u32[]{:S(2)}) copy-start(f32[2,128]{1,0:T(2,128)S(1)} %constant_dynamic-slice_fusion) | copy-start | bytes 3076
  110.6 3.5 copy-start.3
  114.1 54.6 %copy-start.12 = (f32[2,128,176]{1,2,0:T(8,128)}, f32[2,128,176]{1,2,0:T(8,128)S(1)}, u32[]{:S(2)}) copy-start(f32[2,128,176]{1,2,0:T(8,128)S(1)} %fusion.34) | copy-start | bytes 540676
  115.1 54.5 %copy-start.14 = (f32[2,128,176]{1,2,0:T(8,128)}, f32[2,128,176]{1,2,0:T(8,128)S(1)}, u32[]{:S(2)}) copy-start(f32[2,128,176]{1,2,0:T(8,128)S(1)} %fusion.35) | copy-start | bytes 540676
  168.8 4.0 copy-start.17
  168.8 4.0 copy-start.19
  168.8 1.9 copy-start.8
  172.8 91.6 %copy-start.6 = (bf16[128,4096]{1,0:T(8,128)(2,1)S(1)}, bf16[128,4096]{1,0:T(8,128)(2,1)}, u32[]{:S(2)}) copy-start(bf16[128,4096]{1,0:T(8,128)(2,1)} %param.20) | copy-start | bytes 3145732
  248.6 15.6 %all-to-all-start.2 = ((bf16[16,2,2,4096]{3,2,1,0:T(2,128)(2,1)}), bf16[16,2,2,4096]{3,2,1,0:T(2,128)(2,1)S(1)}, u32[]{:S(2)}, u32[]{:S(2)}) async-start(bf16[16,2,2,4096]{3,2,1,0:T(2,128)(2,1)} %reshape.309), calls=%async_computation.3 | async-start | bytes 1048576 | tf_op jit(solution)/shard_map/all_to_all | solution.py:204
  271.7 5.3 copy-start.16
  271.7 230.0 %copy-start.25 = (bf16[128,4096]{1,0:T(8,128)(2,1)S(1)}, bf16[128,4096]{1,0:T(8,128)(2,1)}, u32[]{:S(2)}) copy-start(bf16[128,4096]{1,0:T(8,128)(2,1)} %param.31) | copy-start | bytes 3145732
  271.7 230.0 %all-to-all-start.3 = ((bf16[16,128,4096]{2,1,0:T(8,128)(2,1)}), bf16[16,128,4096]{2,1,0:T(8,128)(2,1)}, u32[]{:S(2)}, u32[]{:S(2)}) async-start(bf16[16,128,4096]{2,1,0:T(8,128)(2,1)} %stack.2), calls=%async_computation.4 | async-start | bytes 33554432 | tf_op jit(solution)/shard_map/all_to_all | solution.py:222
  277.0 308.0 %all-gather.11.cloned.1.call-start = ((), (), s32[]{:S(2)}) async-start(), calls=%async_computation.13 | async-start | bytes 4718592 | tf_op jit(solution)/shard_map/all_gather | solution.py:238
  513.9 142.7 %all-gather.9.cloned.1.call-start = ((), (), s32[]{:S(2)}) async-start(), calls=%async_computation.12 | async-start | bytes 4718592 | tf_op jit(solution)/shard_map/all_gather | solution.py:237
  514.5 446.6 %reduce-scatter.13.cloned.1.call-start = ((), (), s32[]{:S(2)}) async-start(), calls=%async_computation.15 | async-start | bytes 36864
  515.9 446.5 %reduce-scatter.9.cloned.1.call-start = ((), (), s32[]{:S(2)}) async-start(), calls=%async_computation.11 | async-start | bytes 1179648 | tf_op jit(solution)/shard_map/reduce_scatter | solution.py:228
  561.0 472.1 %reduce-scatter.11.cloned.1.call-start = ((), (), s32[]{:S(2)}) async-start(), calls=%async_computation.14 | async-start | bytes 4718592 | tf_op jit(solution)/shard_map/reduce_scatter | solution.py:244
  591.5 67.4 %copy-start.7 = (bf16[2048,128]{1,0:T(8,128)(2,1)S(1)}, bf16[2048,128]{1,0:T(8,128)(2,1)}, u32[]{:S(2)}) copy-start(bf16[2048,128]{1,0:T(8,128)(2,1)} %param.27) | copy-start | bytes 1572868
  669.5 4.9 copy-start.26
  674.4 8.4 copy-start.21
  682.8 6.9 copy-start.27
  689.6 3.5 copy-start.22
  703.6 4.9 copy-start.26
  708.5 8.4 copy-start.21
  716.8 6.9 copy-start.27
  723.7 3.5 copy-start.22
  739.2 4.9 copy-start.26
  744.0 8.4 copy-start.21
  752.4 6.9 copy-start.27
  759.3 3.5 copy-start.22
  774.7 4.9 copy-start.26
  779.6 8.4 copy-start.21
  788.0 6.9 copy-start.27
  794.9 3.5 copy-start.22
  810.3 4.9 copy-start.26
  815.2 8.4 copy-start.21
  823.6 6.9 copy-start.27
  830.4 3.5 copy-start.22
  845.9 4.9 copy-start.26
  850.7 8.4 copy-start.21
  859.1 6.9 copy-start.27
  866.0 3.5 copy-start.22
  881.4 4.9 copy-start.26
  886.3 8.4 copy-start.21
  894.7 6.9 copy-start.27
  901.5 3.5 copy-start.22
  917.0 4.9 copy-start.26
  921.8 8.4 copy-start.21
  930.2 6.9 copy-start.27
  937.1 3.5 copy-start.22
  951.9 4.1 copy-start.18
  953.5 2.5 copy-start.5
  953.5 5.0 copy-start.10
  953.5 5.0 copy-start.13
  953.5 5.0 copy-start.15
  953.5 5.0 copy-start.24
  956.0 77.1 %copy-start.1 = (bf16[2,4096,176]{1,2,0:T(8,128)(2,1)S(1)}, bf16[2,4096,176]{1,2,0:T(8,128)(2,1)}, u32[]{:S(2)}) copy-start(bf16[2,4096,176]{1,2,0:T(8,128)(2,1)} %param.21) | copy-start | bytes 8650756
  (4 other events, 5.4 us)
Sparse Core Ops, SparseCore 0:
  56.8 53.7 all-gather.6
  113.5 51.8 all-gather.4
  172.9 72.9 reduce-scatter.6
  514.0 70.9 all-gather.10
  587.3 69.3 all-gather.8
  659.8 59.8 reduce-scatter.12
  723.3 70.7 reduce-scatter.8
  952.0 80.9 reduce-scatter.10
